TPU v7x, 32 devices: a whole 2x2x4 slice. The times are simulated.
32 devices in a mesh: rows: 16 (over z, y, x), cols: 2 (over core).
Axes of the slice: x: 2, y: 2, z: 4, core: 2. Of those that a mesh axis runs over, the one named last changes fastest.
Arguments:
- snapshots: bfloat16 [16384, 2, 2, 128], P('rows', 'cols'), may hold values from -12 to 12
- scales: float32 [32, 2, 2], P('rows'), may hold values from 0.2 to 9
Outputs:
- coefficients: float32 [128, 2, 2, 128], P(None, 'cols')
- updated: bfloat16 [16384, 2, 2, 128], P('rows', 'cols')
All inputs are finite; a program needn't handle non-finite values.
Results may differ from a plain program's by a relative error of at most 0.012.
Values may be sent and summed in bfloat16 or wider, within the bound.
No kernel may reach another device: no remote copies, remote signals or barrier semaphores. Data moves between devices by JAX's collectives and lax.ppermute only.
A program may use at most 64 MiB of HBM per device.

v0:
```python
import math
import jax
import jax.numpy as jnp
from jax import lax
from jax.sharding import PartitionSpec as P

HIGH = lax.Precision.HIGHEST


def spread(shard, axis, root):
    mine = lax.axis_index(axis) == root
    return lax.psum(jnp.where(mine, shard, jnp.zeros_like(shard)), axis)


def product(left, right):
    return jnp.dot(left, right, precision=HIGH, preferred_element_type=jnp.float32)


def scaled_values(snapshots, scales, group):
    points, _, rounds, width = snapshots.shape
    nblock = scales.shape[0]
    own_scales = lax.dynamic_slice_in_dim(scales, group, 1, 1)[:, 0, :]
    shaped = snapshots.astype(jnp.float32).reshape(nblock, points // nblock, rounds, width)
    return (shaped * own_scales[:, None, :, None]).reshape(points, rounds * width)


def upper_inverse(gram):
    width = gram.shape[0]
    positions = jnp.arange(width, dtype=jnp.int32)

    def factor_step(column_index, state_pair):
        remaining, lower_factor = state_pair
        picker = (positions == column_index).astype(jnp.float32)
        column = jnp.sum(remaining * picker[None, :], axis=1)
        pivot_value = jnp.sum(column * picker)
        column = jnp.where(positions >= column_index, column / jnp.sqrt(pivot_value), 0.0)
        lower_factor = lower_factor + column[:, None] * picker[None, :]
        remaining = remaining - column[:, None] * column[None, :]
        return (remaining, lower_factor)

    start_lower = jnp.zeros((width, width), jnp.float32)
    _, lower_factor = lax.fori_loop(0, width, factor_step, (gram, start_lower))

    def solve_step(row_index, inverse_rows):
        picker = (positions == row_index).astype(jnp.float32)
        lower_row = jnp.sum(lower_factor * picker[:, None], axis=0)
        diagonal_entry = jnp.sum(lower_row * picker)
        earlier = jnp.where(positions < row_index, lower_row, 0.0)
        new_row = (picker - product(earlier[None, :], inverse_rows)[0]) / diagonal_entry
        return inverse_rows + picker[:, None] * new_row[None, :]

    lower_inverse = lax.fori_loop(0, width, solve_step, jnp.zeros((width, width), jnp.float32))
    return lower_inverse.T


def shards(snapshots, scales):
    points, _, rounds, width = snapshots.shape
    group = lax.axis_index("cols")
    values = scaled_values(snapshots, scales, group)
    panel = values[:, :width]
    gram = lax.psum(product(panel.T, panel), "rows")
    inverse = upper_inverse(gram)
    basis = spread(product(panel, inverse).astype(jnp.bfloat16), "cols", 0).astype(jnp.float32)
    raw = lax.psum(product(basis.T, values), "rows")
    root = math.sqrt(points * lax.axis_size("rows"))
    remainder = values - product(basis, raw)
    leading = jnp.where(group == 0, root * basis, remainder[:, :width])
    whole = jnp.concatenate([leading, remainder[:, width:]], axis=1)
    updated = whole.astype(jnp.bfloat16).reshape(points, 1, rounds, width)
    coefficients = (raw / root).reshape(width, 1, rounds, width)
    return (coefficients, updated)


def solution(mesh):
    return jax.shard_map(
        shards,
        mesh=mesh,
        in_specs=(P("rows", "cols", None, None), P("rows", None, None)),
        out_specs=(P(None, "cols", None, None), P("rows", "cols", None, None)),
        check_vma=False,
    )
```

profile of v0, /device:TPU:0, one launch (start us, length us, event | category | flops | bytes accessed | tf_op | source)
XLA Modules:
  0.0 862.3 jit_solution(12025838508278605038)
XLA Ops:
  7.2 1.1 bitcast_convert_fusion
  8.9 1.7 fusion.19
  10.6 108.1 %all-reduce.4.cloned.1.call-done = f32[128,128]{1,0:T(8,128)} async-done(((f32[128,128]{1,0:T(8,128)}), f32[128,128]{1,0:T(8,128)}) %all-reduce.4.cloned.1.call-update) | async-done | bytes 65552 | tf_op jit(solution)/shard_map/psum | solution.py:61
  118.8 393.0 %while.32 = (s32[]{:T(128)}, f32[128,128]{1,0:T(8,128)}, f32[128,128]{1,0:T(8,128)S(1)}, s32[]{:T(128)}, s32[]{:T(128)}) while((s32[]{:T(128)}, f32[128,128]{1,0:T(8,128)}, f32[128,128]{1,0:T(8,128)S(1)}, s32[]{:T(128)}, s32[]{:T(128)}) %tuple.74), condition=%wide.region_4.5_spmd.clone.clone, body=%wide.region_1.4_spmd.clone.clone.sunk | while | flops 115586 | bytes 856219 | solution.py:42
  118.8 1.0 multiply_reduce_fusion.4
  121.8 1.0 multiply_reduce_fusion.4
  124.9 1.0 multiply_reduce_fusion.4
  128.0 1.0 multiply_reduce_fusion.4
  131.1 1.0 multiply_reduce_fusion.4
  134.1 1.0 multiply_reduce_fusion.4
  137.2 1.0 multiply_reduce_fusion.4
  140.3 1.0 multiply_reduce_fusion.4
  143.3 1.0 multiply_reduce_fusion.4
  146.4 1.0 multiply_reduce_fusion.4
  149.5 1.0 multiply_reduce_fusion.4
  152.5 1.0 multiply_reduce_fusion.4
  155.6 1.0 multiply_reduce_fusion.4
  158.7 1.0 multiply_reduce_fusion.4
  161.8 1.0 multiply_reduce_fusion.4
  164.8 1.0 multiply_reduce_fusion.4
  167.9 1.0 multiply_reduce_fusion.4
  171.0 1.0 multiply_reduce_fusion.4
  174.0 1.0 multiply_reduce_fusion.4
  177.1 1.0 multiply_reduce_fusion.4
  180.2 1.0 multiply_reduce_fusion.4
  183.2 1.0 multiply_reduce_fusion.4
  186.3 1.0 multiply_reduce_fusion.4
  189.4 1.0 multiply_reduce_fusion.4
  192.5 1.0 multiply_reduce_fusion.4
  195.5 1.0 multiply_reduce_fusion.4
  198.6 1.0 multiply_reduce_fusion.4
  201.7 1.0 multiply_reduce_fusion.4
  204.7 1.0 multiply_reduce_fusion.4
  207.8 1.0 multiply_reduce_fusion.4
  210.9 1.0 multiply_reduce_fusion.4
  213.9 1.0 multiply_reduce_fusion.4
  217.0 1.0 multiply_reduce_fusion.4
  220.1 1.0 multiply_reduce_fusion.4
  223.2 1.0 multiply_reduce_fusion.4
  226.2 1.0 multiply_reduce_fusion.4
  229.3 1.0 multiply_reduce_fusion.4
  232.4 1.0 multiply_reduce_fusion.4
  511.7 210.5 %while.33 = (s32[]{:T(128)}, f32[128,128]{1,0:T(8,128)S(1)}, f32[128,128]{1,0:T(8,128)S(1)}, s32[]{:T(128)}, s32[]{:T(128)}) while((s32[]{:T(128)}, f32[128,128]{1,0:T(8,128)S(1)}, f32[128,128]{1,0:T(8,128)S(1)}, s32[]{:T(128)}, s32[]{:T(128)}) %tuple.77), condition=%wide.region_8.9_spmd.clone.clone, body=%wide.region_5.8_spmd.clone.clone.sunk | while | flops 296194 | bytes 266332 | solution.py:52
  722.2 1.3 fusion.16
  723.6 17.4 %all-reduce.6.cloned.1.call-done = bf16[1024,128]{1,0:T(8,128)(2,1)} async-done(((bf16[1024,128]{1,0:T(8,128)(2,1)}), bf16[1024,128]{1,0:T(8,128)(2,1)}) %all-reduce.6.cloned.1.call-update) | async-done | bytes 262160 | tf_op jit(solution)/shard_map/psum | solution.py:12
  741.0 2.3 fusion.21
  743.3 109.1 %all-reduce.8.cloned.1.call-done = f32[128,256]{1,0:T(8,128)} async-done(((f32[128,256]{1,0:T(8,128)}), f32[128,256]{1,0:T(8,128)}) %all-reduce.8.cloned.1.call-update) | async-done | bytes 131088 | tf_op jit(solution)/shard_map/psum | solution.py:64
  852.4 1.5 convolution_subtract_fusion
  (1776 shorter events, 468.9 us)
Async XLA Ops:
  7.2 111.6 %all-reduce.4.cloned.1.call-start = ((), (), s32[]{:S(2)}) async-start(), calls=%async_computation | async-start | bytes 131072 | tf_op jit(solution)/shard_map/psum | solution.py:61
  10.6 730.5 %all-reduce.6.cloned.1.call-start = ((), (), s32[]{:S(2)}) async-start(), calls=%async_computation.1 | async-start | bytes 524288 | tf_op jit(solution)/shard_map/psum | solution.py:12
  118.8 2.3 copy-start.1
  121.8 2.3 copy-start.1
  124.9 2.3 copy-start.1
  128.0 2.3 copy-start.1
  131.1 2.3 copy-start.1
  134.1 2.3 copy-start.1
  137.2 2.3 copy-start.1
  140.3 2.3 copy-start.1
  143.3 2.3 copy-start.1
  146.4 2.3 copy-start.1
  149.5 2.3 copy-start.1
  152.5 2.3 copy-start.1
  155.6 2.3 copy-start.1
  158.7 2.3 copy-start.1
  161.8 2.3 copy-start.1
  164.8 2.3 copy-start.1
  167.9 2.3 copy-start.1
  171.0 2.3 copy-start.1
  174.0 2.3 copy-start.1
  177.1 2.3 copy-start.1
  180.2 2.3 copy-start.1
  183.2 2.3 copy-start.1
  186.3 2.3 copy-start.1
  189.4 2.3 copy-start.1
  192.5 2.3 copy-start.1
  195.5 2.3 copy-start.1
  198.6 2.3 copy-start.1
  201.7 2.3 copy-start.1
  204.7 2.3 copy-start.1
  207.8 2.3 copy-start.1
  210.9 2.3 copy-start.1
  213.9 2.3 copy-start.1
  217.0 2.3 copy-start.1
  220.1 2.3 copy-start.1
  223.2 2.3 copy-start.1
  226.2 2.3 copy-start.1
  229.3 2.3 copy-start.1
  232.4 2.3 copy-start.1
  235.4 2.3 copy-start.1
  238.5 2.3 copy-start.1
  241.6 2.3 copy-start.1
  244.6 2.3 copy-start.1
  247.7 2.3 copy-start.1
  250.8 2.3 copy-start.1
  723.6 128.9 %all-reduce.8.cloned.1.call-start = ((), (), s32[]{:S(2)}) async-start(), calls=%async_computation.2 | async-start | bytes 262144 | tf_op jit(solution)/shard_map/psum | solution.py:64
  741.0 111.4 %copy-start.3 = (bf16[1024,128]{1,0:T(8,128)(2,1)S(1)}, bf16[1024,128]{1,0:T(8,128)(2,1)}, u32[]{:S(2)}) copy-start(bf16[1024,128]{1,0:T(8,128)(2,1)} %all-reduce.6.cloned.1.call-done) | copy-start | bytes 786436
  (214 other events, 278.2 us)
Sparse Core Ops, SparseCore 0:
  14.1 104.6 all-reduce.3
  723.7 17.3 all-reduce.5
  747.1 105.3 all-reduce.7
where the time goes:
time: 871 us; the launch traced here: 862 us
  other arithmetic  326 us (37%)
  waiting for transfers between devices  235 us (27%)
  matrix products  109 us (13%)
  loops' own time  98.7 us (11%)
  local copies, waits for them, and re-layouts  80.3 us (9%)
  between operations  13.9 us (2%)
    reduce_sum x128, other arithmetic, factor_step(): column = jnp.sum(remaining * picker[None, :], axis=1)  129 us
    psum x1, waiting for transfers between devices, shards(): raw = lax.psum(product(basis.T, values), 'rows')  109 us
    dot_general x132, matrix products, product(): jnp.dot(left, right, precision=HIGH, preferred_element_type=jnp.float32)  109 us
    psum x1, waiting for transfers between devices, shards(): gram = lax.psum(product(panel.T, panel), 'rows')  108 us
    another operation x1, loops' own time, upper_inverse(): _, lower_factor = lax.fori_loop(0, width, factor_step, (gram, start_lower))  94.7 us
    while x512, local copies, waits for them, and re-layouts  78.3 us
    reduce_sum x128, other arithmetic, factor_step(): pivot_value = jnp.sum(column * picker)  78.3 us
    reduce_sum x128, other arithmetic, solve_step(): diagonal_entry = jnp.sum(lower_row * picker)  78.1 us
  transfers between devices with their start and end apart: 3, of which 3 were waited for; matrix products, arithmetic and copies ran while one was open for 0% of the time, Pallas kernels for 0%

commit v1 on v0

--- a/solution.py
+++ b/solution.py
@@ -9,7 +9,7 @@
 
 def spread(shard, axis, root):
     mine = lax.axis_index(axis) == root
-    return lax.psum(jnp.where(mine, shard, jnp.zeros_like(shard)), axis)
+    return jnp.sum(lax.all_gather(jnp.where(mine, shard, jnp.zeros_like(shard)), axis_name=axis), 0)
 
 
 def product(left, right):

time: 871 us -> 849 us (0.975)
  waiting for transfers between devices: 235 us -> 212 us
    psum x1 -> x0, waiting for transfers between devices: 17.4 us -> none  [spread(): return lax.psum(jnp.where(mine, shard, jnp.zeros_like(shard)), axis)]
  transfers between devices with their start and end apart: 3 -> 2, of which waited for: 3 -> 2; matrix products, arithmetic and copies ran while one was open for 0% -> 0% of each run, Pallas kernels for 0% -> 0%
where the time goes in v1:
time: 849 us; the launch traced here: 840 us
  other arithmetic  326 us (38%)
  waiting for transfers between devices  212 us (25%)
  matrix products  107 us (13%)
  loops' own time  98.7 us (12%)
  local copies, waits for them, and re-layouts  80.3 us (9%)
  between operations  14.2 us (2%)
    reduce_sum x128, other arithmetic, factor_step(): column = jnp.sum(remaining * picker[None, :], axis=1)  129 us
    psum x1, waiting for transfers between devices, shards(): gram = lax.psum(product(panel.T, panel), 'rows')  108 us
    dot_general x132, matrix products, product(): jnp.dot(left, right, precision=HIGH, preferred_element_type=jnp.float32)  107 us
    psum x1, waiting for transfers between devices, shards(): raw = lax.psum(product(basis.T, values), 'rows')  103 us
    another operation x1, loops' own time, upper_inverse(): _, lower_factor = lax.fori_loop(0, width, factor_step, (gram, start_lower))  94.7 us
    while x512, local copies, waits for them, and re-layouts  78.3 us
    reduce_sum x128, other arithmetic, factor_step(): pivot_value = jnp.sum(column * picker)  78.3 us
    reduce_sum x128, other arithmetic, solve_step(): diagonal_entry = jnp.sum(lower_row * picker)  78.1 us
  transfers between devices with their start and end apart: 2, of which 2 were waited for; matrix products, arithmetic and copies ran while one was open for 0% of the time, Pallas kernels for 0%

profile of v1, /device:TPU:0, one launch (start us, length us, event | category | flops | bytes accessed | tf_op | source)
XLA Modules:
  0.0 840.1 jit_solution(7264948017639785124)
XLA Ops:
  7.2 1.1 bitcast_convert_fusion
  8.9 1.7 fusion.19
  10.6 108.1 %all-reduce.3.cloned.1.call-done = f32[128,128]{1,0:T(8,128)} async-done(((f32[128,128]{1,0:T(8,128)}), f32[128,128]{1,0:T(8,128)}) %all-reduce.3.cloned.1.call-update) | async-done | bytes 65552 | tf_op jit(solution)/shard_map/psum | solution.py:61
  118.8 393.0 %while.32 = (s32[]{:T(128)}, f32[128,128]{1,0:T(8,128)}, f32[128,128]{1,0:T(8,128)S(1)}, s32[]{:T(128)}, s32[]{:T(128)}) while((s32[]{:T(128)}, f32[128,128]{1,0:T(8,128)}, f32[128,128]{1,0:T(8,128)S(1)}, s32[]{:T(128)}, s32[]{:T(128)}) %tuple.74), condition=%wide.region_4.5_spmd.clone.clone, body=%wide.region_1.4_spmd.clone.clone.sunk | while | flops 115586 | bytes 856219 | solution.py:42
  118.8 1.0 multiply_reduce_fusion.4
  121.8 1.0 multiply_reduce_fusion.4
  124.9 1.0 multiply_reduce_fusion.4
  128.0 1.0 multiply_reduce_fusion.4
  131.1 1.0 multiply_reduce_fusion.4
  134.1 1.0 multiply_reduce_fusion.4
  137.2 1.0 multiply_reduce_fusion.4
  140.3 1.0 multiply_reduce_fusion.4
  143.3 1.0 multiply_reduce_fusion.4
  146.4 1.0 multiply_reduce_fusion.4
  149.5 1.0 multiply_reduce_fusion.4
  152.5 1.0 multiply_reduce_fusion.4
  155.6 1.0 multiply_reduce_fusion.4
  158.7 1.0 multiply_reduce_fusion.4
  161.8 1.0 multiply_reduce_fusion.4
  164.8 1.0 multiply_reduce_fusion.4
  167.9 1.0 multiply_reduce_fusion.4
  171.0 1.0 multiply_reduce_fusion.4
  174.0 1.0 multiply_reduce_fusion.4
  177.1 1.0 multiply_reduce_fusion.4
  180.2 1.0 multiply_reduce_fusion.4
  183.2 1.0 multiply_reduce_fusion.4
  186.3 1.0 multiply_reduce_fusion.4
  189.4 1.0 multiply_reduce_fusion.4
  192.5 1.0 multiply_reduce_fusion.4
  195.5 1.0 multiply_reduce_fusion.4
  198.6 1.0 multiply_reduce_fusion.4
  201.7 1.0 multiply_reduce_fusion.4
  204.7 1.0 multiply_reduce_fusion.4
  207.8 1.0 multiply_reduce_fusion.4
  210.9 1.0 multiply_reduce_fusion.4
  213.9 1.0 multiply_reduce_fusion.4
  217.0 1.0 multiply_reduce_fusion.4
  220.1 1.0 multiply_reduce_fusion.4
  223.2 1.0 multiply_reduce_fusion.4
  226.2 1.0 multiply_reduce_fusion.4
  229.3 1.0 multiply_reduce_fusion.4
  232.4 1.0 multiply_reduce_fusion.4
  235.4 1.0 multiply_reduce_fusion.4
  511.7 210.5 %while.33 = (s32[]{:T(128)}, f32[128,128]{1,0:T(8,128)S(1)}, f32[128,128]{1,0:T(8,128)S(1)}, s32[]{:T(128)}, s32[]{:T(128)}) while((s32[]{:T(128)}, f32[128,128]{1,0:T(8,128)S(1)}, f32[128,128]{1,0:T(8,128)S(1)}, s32[]{:T(128)}, s32[]{:T(128)}) %tuple.77), condition=%wide.region_8.9_spmd.clone.clone, body=%wide.region_5.8_spmd.clone.clone.sunk | while | flops 296194 | bytes 266332 | solution.py:52
  722.8 2.2 all-gather
  725.2 1.2 fusion.21
  726.5 103.5 %all-reduce.5.cloned.1.call-done = f32[128,256]{1,0:T(8,128)} async-done(((f32[128,256]{1,0:T(8,128)}), f32[128,256]{1,0:T(8,128)}) %all-reduce.5.cloned.1.call-update) | async-done | bytes 131088 | tf_op jit(solution)/shard_map/psum | solution.py:64
  829.9 1.5 convolution_subtract_fusion
  (1773 shorter events, 468.7 us)
Async XLA Ops:
  7.2 111.6 %all-reduce.3.cloned.1.call-start = ((), (), s32[]{:S(2)}) async-start(), calls=%async_computation | async-start | bytes 131072 | tf_op jit(solution)/shard_map/psum | solution.py:61
  10.6 819.4 %all-reduce.5.cloned.1.call-start = ((), (), s32[]{:S(2)}) async-start(), calls=%async_computation.1 | async-start | bytes 262144 | tf_op jit(solution)/shard_map/psum | solution.py:64
  118.8 2.3 copy-start.1
  121.8 2.3 copy-start.1
  124.9 2.3 copy-start.1
  128.0 2.3 copy-start.1
  131.1 2.3 copy-start.1
  134.1 2.3 copy-start.1
  137.2 2.3 copy-start.1
  140.3 2.3 copy-start.1
  143.3 2.3 copy-start.1
  146.4 2.3 copy-start.1
  149.5 2.3 copy-start.1
  152.5 2.3 copy-start.1
  155.6 2.3 copy-start.1
  158.7 2.3 copy-start.1
  161.8 2.3 copy-start.1
  164.8 2.3 copy-start.1
  167.9 2.3 copy-start.1
  171.0 2.3 copy-start.1
  174.0 2.3 copy-start.1
  177.1 2.3 copy-start.1
  180.2 2.3 copy-start.1
  183.2 2.3 copy-start.1
  186.3 2.3 copy-start.1
  189.4 2.3 copy-start.1
  192.5 2.3 copy-start.1
  195.5 2.3 copy-start.1
  198.6 2.3 copy-start.1
  201.7 2.3 copy-start.1
  204.7 2.3 copy-start.1
  207.8 2.3 copy-start.1
  210.9 2.3 copy-start.1
  213.9 2.3 copy-start.1
  217.0 2.3 copy-start.1
  220.1 2.3 copy-start.1
  223.2 2.3 copy-start.1
  226.2 2.3 copy-start.1
  229.3 2.3 copy-start.1
  232.4 2.3 copy-start.1
  235.4 2.3 copy-start.1
  238.5 2.3 copy-start.1
  241.6 2.3 copy-start.1
  244.6 2.3 copy-start.1
  247.7 2.3 copy-start.1
  250.8 2.3 copy-start.1
  253.9 2.3 copy-start.1
  256.9 2.3 copy-start.1
  (212 other events, 273.6 us)
Sparse Core Ops, SparseCore 0:
  14.1 104.6 all-reduce.2
  726.6 103.2 all-reduce.4
